TPU v7x, 32 devices: a whole 2x2x4 slice. The times are simulated.
32 devices in a mesh: space: 8 (over z, y), freq: 4 (over x, core).
Axes of the slice: x: 2, y: 2, z: 4, core: 2. Of those that a mesh axis runs over, the one named last changes fastest.
Arguments:
- forcing: bfloat16 [4, 32, 8, 8, 1536], P(None, 'freq', None, 'space'), may hold values from -36 to 36
- base_harm: float32 [7, 2, 8, 1536], P(None, None, 'space'), may hold values from -6 to 6
- mixing: float32 [7, 4, 4], replicated, may hold values from -3 to 3
- mean_flow: float32 [1536], replicated, may hold values from 0.2 to 1.2
- harm_lo: int32 [1], replicated, may hold values from -20 to -9
- couple_flags: int32 [32, 7], P('freq'), may hold values 0 or 1
Outputs:
- response: bfloat16 [4, 32, 8, 8, 1536], P(None, 'freq', None, 'space')
- gram_matrix: float32 [4, 4], replicated
All inputs are finite; a program needn't handle non-finite values. No bound on the sum of `couple_flags` on one device may be relied on, other than what follows from the above.
Results may differ from a plain program's by a relative error of at most 0.004.
Values may be sent and summed in bfloat16 or wider, within the bound.
No kernel may reach another device: no remote copies, remote signals or barrier semaphores. Data moves between devices by JAX's collectives and lax.ppermute only.
A program may use at most 128 MiB of HBM per device.

v0:
```python
import jax
import jax.numpy as jnp
from jax import lax
from jax.sharding import PartitionSpec as P

V = 4
NY = 32
NZ = 48
OMEGA = 0.05
VISCOSITY = 0.25


def passed_along(value, axis, by):
    devices = lax.axis_size(axis)
    pairs = [(i, i + by) for i in range(devices) if 0 <= i + by < devices]
    return lax.ppermute(value, axis, pairs)


def with_halo(cells, sides, width):
    for axis, dim in sides:
        count = lax.axis_size(axis)
        ends = count - 1
        head = lax.slice_in_dim(cells, 0, width, axis=dim)
        tail = lax.slice_in_dim(cells, cells.shape[dim] - width, cells.shape[dim], axis=dim)
        cells = jnp.concatenate(
            [
                lax.ppermute(tail, axis, [(i, (i + 1) % count) for i in range(ends)]),
                cells,
                lax.ppermute(head, axis, [((i + 1) % count, i) for i in range(ends)]),
            ],
            axis=dim,
        )
    return cells


def crossflow(values):
    cells = NY * NZ
    position = jnp.arange(cells, dtype=jnp.int32)
    span_pos = position % NZ
    wake_pos = position // NZ
    span_up = jnp.where(span_pos == NZ - 1, jnp.roll(values, NZ - 1, -1), jnp.roll(values, -1, -1))
    span_down = jnp.where(span_pos == 0, jnp.roll(values, 1 - NZ, -1), jnp.roll(values, 1, -1))
    wake_up = jnp.where(wake_pos == NY - 1, 0.0, jnp.roll(values, -NZ, -1))
    wake_down = jnp.where(wake_pos == 0, 0.0, jnp.roll(values, NZ, -1))
    return VISCOSITY * (wake_up + wake_down + span_up + span_down - 6.0 * values)


def streamwise(left_vals, right_vals, stream):
    return (VISCOSITY + 0.5 * stream) * left_vals + (VISCOSITY - 0.5 * stream) * right_vals


def rotation(values, frequency):
    spin_rate = (OMEGA * frequency)[:, None, None, None]
    real_part = values[..., :V, :, :]
    imag_part = values[..., V:, :, :]
    return jnp.concatenate([-spin_rate * imag_part, spin_rate * real_part], axis=-3)


def coupling(padded, base_modes, mixing, couplers):
    count_h = couplers.shape[0]
    summed = None
    for j in range(7):
        offset = j - 3
        source = lax.slice_in_dim(padded, 3 - offset, 3 - offset + count_h, axis=padded.ndim - 4)
        halves = source.reshape(source.shape[:-3] + (2, V) + source.shape[-2:])
        blended = jnp.einsum(
            "vw,...cwxn->...cvxn", mixing[j], halves, precision=lax.Precision.HIGHEST
        )
        base_re = base_modes[j, 0]
        base_im = base_modes[j, 1]
        mix_re = blended[..., 0, :, :, :]
        mix_im = blended[..., 1, :, :, :]
        product_term = jnp.stack(
            [base_re * mix_re - base_im * mix_im, base_re * mix_im + base_im * mix_re], axis=-4
        )
        weights = couplers[:, j].astype(jnp.float32)[:, None, None, None, None]
        contrib = weights * product_term
        summed = contrib if summed is None else summed + contrib
    return summed.reshape(summed.shape[:-5] + (count_h, 2 * V) + summed.shape[-2:])


def local(forcing, base_harm, mixing, mean_flow, harm_lo, couple_flags):
    count_h = forcing.shape[1]
    planes = forcing.shape[3]
    widened = forcing.astype(jnp.float32)
    zero_plane = jnp.zeros_like(widened)
    left_vals = jnp.concatenate([zero_plane, widened[:, :, :, :-1, :]], axis=3)
    right_vals = jnp.concatenate([widened[:, :, :, 1:, :], zero_plane], axis=3)
    interior = streamwise(left_vals, right_vals, mean_flow)
    going_right = (VISCOSITY + 0.5 * mean_flow) * widened
    going_left = (VISCOSITY - 0.5 * mean_flow) * widened
    from_left = passed_along(going_right.astype(jnp.bfloat16), "space", 1).astype(going_right.dtype)
    from_right = passed_along(going_left.astype(jnp.bfloat16), "space", -1).astype(going_left.dtype)
    along_x = interior + from_left + from_right
    spatial = crossflow(widened) + along_x
    rim_block = with_halo(forcing, (("freq", 1),), 3)
    padded = rim_block.astype(jnp.float32)
    start_k = lax.axis_index("freq") * count_h
    frequency = (harm_lo[0] + start_k + jnp.arange(count_h, dtype=jnp.int32)).astype(jnp.float32)
    result = (
        rotation(widened, frequency) - spatial - coupling(padded, base_harm, mixing, couple_flags)
    )
    response = result.astype(jnp.bfloat16)
    flattened = response.reshape(response.shape[0], -1)
    cells_all = (
        count_h
        * lax.axis_size("freq")
        * forcing.shape[2]
        * planes
        * lax.axis_size("space")
        * forcing.shape[4]
    )
    partial_value = jnp.dot(flattened, flattened.T, preferred_element_type=jnp.float32) / cells_all
    gram_matrix = lax.psum(partial_value, "space")
    gram_matrix = lax.psum(gram_matrix, "freq")
    return (response, gram_matrix)


def solution(mesh):
    return jax.shard_map(
        local,
        mesh=mesh,
        in_specs=(
            P(None, "freq", None, "space", None),
            P(None, None, "space", None),
            P(),
            P(),
            P(),
            P("freq", None),
        ),
        out_specs=(P(None, "freq", None, "space", None), P()),
        check_vma=False,
    )
```

profile of v0, /device:TPU:0, one launch (start us, length us, event | category | flops | bytes accessed | tf_op | source)
XLA Modules:
  0.0 122.0 jit_solution(8223498740401340326)
XLA Ops:
  0.6 1.2 fusion.35
  1.8 1.3 %collective-permute-start.2 = (bf16[4,3,8,1,1536]{4,2,3,1,0:T(8,128)(2,1)S(1)}, bf16[4,3,8,1,1536]{4,2,3,1,0:T(8,128)(2,1)S(1)}, u32[]{:S(2)}, u32[]{:S(2)}) collective-permute-start(bf16[4,3,8,1,1536]{4,2,3,1,0:T(8,128)(2,1)S(1)} %get-tuple-element.54), channel_id=1, source_target_pairs={{1,0},{2,1},{3,2},{5,4},{6,5},{7,6},{9,8},{10,9},{11,10},{13,12},{... | collective-permute-start | bytes 884744 | tf_op jit(solution)/shard_map/ppermute | solution.py:29
  3.1 3.0 %collective-permute-start.3 = (bf16[4,3,8,1,1536]{4,2,3,1,0:T(8,128)(2,1)S(1)}, bf16[4,3,8,1,1536]{4,2,3,1,0:T(8,128)(2,1)S(1)}, u32[]{:S(2)}, u32[]{:S(2)}) collective-permute-start(bf16[4,3,8,1,1536]{4,2,3,1,0:T(8,128)(2,1)S(1)} %get-tuple-element.55), channel_id=1, source_target_pairs={{0,1},{1,2},{2,3},{4,5},{5,6},{6,7},{8,9},{9,10},{10,11},{12,13},{... | collective-permute-start | bytes 884744 | tf_op jit(solution)/shard_map/ppermute | solution.py:27
  6.2 1.3 %add_multiply_fusion = (f32[1536]{0:T(1024)}, f32[1536]{0:T(1024)S(1)}, f32[1536]{0:T(1024)S(1)}) fusion(f32[1536]{0:T(1024)} %param.9), kind=kLoop, calls=%fused_computation.78 | loop fusion | flops 7680 | bytes 24576 | tf_op jit(solution)/shard_map/add | solution.py:49
  7.5 1.4 %multiply_convert_fusion.1 = (bf16[4,8,8,1,1536]{4,2,3,1,0:T(8,128)(2,1)}, bf16[4,8,8,1,1536]{4,2,3,1,0:T(8,128)(2,1)}) fusion(bf16[4,8,8,1,1536]{4,2,3,1,0:T(8,128)(2,1)S(1)} %copy-done, f32[1536]{0:T(1024)S(1)} %get-tuple-element.73, f32[1536]{0:T(1024)S(1)} %get-tuple-element.72), kind=kLoop, calls=%fused_computation.41 | loop fusion | flops 1966080 | bytes 2371584 | tf_op jit(solution)/shard_map/convert_element_type | solution.py:92
  8.9 5.8 %collective-permute-start = (bf16[4,8,8,1,1536]{4,2,3,1,0:T(8,128)(2,1)}, bf16[4,8,8,1,1536]{4,2,3,1,0:T(8,128)(2,1)}, u32[]{:S(2)}, u32[]{:S(2)}) collective-permute-start(bf16[4,8,8,1,1536]{4,2,3,1,0:T(8,128)(2,1)} %get-tuple-element.52), channel_id=1, source_target_pairs={{0,4},{4,8},{8,12},{12,16},{16,20},{20,24},{24,28},{1,5},{5,9},{9,... | collective-permute-start | bytes 2359304 | tf_op jit(solution)/shard_map/ppermute | solution.py:16
  14.7 1.3 %collective-permute-start.1 = (bf16[4,8,8,1,1536]{4,2,3,1,0:T(8,128)(2,1)}, bf16[4,8,8,1,1536]{4,2,3,1,0:T(8,128)(2,1)}, u32[]{:S(2)}, u32[]{:S(2)}) collective-permute-start(bf16[4,8,8,1,1536]{4,2,3,1,0:T(8,128)(2,1)} %get-tuple-element.53), channel_id=1, source_target_pairs={{4,0},{8,4},{12,8},{16,12},{20,16},{24,20},{28,24},{5,1},{9,5},{13... | collective-permute-start | bytes 2359304 | tf_op jit(solution)/shard_map/ppermute | solution.py:16
  16.0 0.6 broadcast_compare_fusion
  16.6 0.6 fusion.22
  17.2 0.7 fusion.39
  17.9 0.7 fusion.36
  18.7 0.2 reshape.596
  18.9 2.1 %fusion.38 = (f32[4,8,8,1,1489]{4,2,3,1,0:T(8,128)}, f32[4,8,8,1,1489]{4,2,3,1,0:T(8,128)}) fusion(bf16[4,8,8,1,1536]{4,2,3,1,0:T(8,128)(2,1)S(1)} %copy-done), kind=kLoop, calls=%fused_computation.125 | loop fusion | bytes 6098944 | tf_op jit(solution)/shard_map/jit(_roll_static)/slice | solution.py:42
  21.0 2.1 %fusion.41 = (f32[4,8,8,1,1488]{4,2,3,1,0:T(8,128)}, f32[4,8,8,1,1488]{4,2,3,1,0:T(8,128)}) fusion(bf16[4,8,8,1,1536]{4,2,3,1,0:T(8,128)(2,1)S(1)} %copy-done), kind=kLoop, calls=%fused_computation.128 | loop fusion | bytes 6094848 | tf_op jit(solution)/shard_map/jit(_roll_static)/slice | solution.py:44
  23.1 2.1 %fusion.37 = (f32[4,8,8,1,1535]{4,2,3,1,0:T(8,128)}, f32[4,8,8,1,1535]{4,2,3,1,0:T(8,128)}) fusion(bf16[4,8,8,1,1536]{4,2,3,1,0:T(8,128)(2,1)S(1)} %copy-done), kind=kLoop, calls=%fused_computation.124 | loop fusion | bytes 6287360 | tf_op jit(solution)/shard_map/jit(_roll_static)/slice | solution.py:42
  25.8 0.8 convert_reduce_fusion.6
  26.6 0.8 slice_reduce_fusion.6
  27.4 0.2 slice_reduce_fusion.20
  27.6 2.6 %convolution_bitcast_fusion.3 = f32[4,8,2,4,1,1536]{5,3,2,1,0,4:T(4,128)} fusion(bf16[4,8,2,4,1536]{4,3,2,1,0:T(4,128)(2,1)S(1)} %reshape.596, f32[4,4]{1,0:T(4,128)S(1)} %get-tuple-element.18), kind=kOutput, calls=%fused_computation.3 | convolution fusion | flops 18874368 | bytes 2359360 | tf_op jit(solution)/shard_map/vw,...cwxn->...cvxn/dot_general | solution.py:66
  30.2 0.6 convert_multiply_fusion
  30.8 0.7 fusion.40
  31.5 0.0 collective-permute-done.3
  31.6 1.5 %constant_dynamic-update-slice_fusion.1 = (bf16[4,11,8,1,1536]{4,2,3,1,0:T(8,128)(2,1)S(1)}, f32[4,8,8,1,1536]{4,2,3,1,0:T(8,128)}, bf16[4,11,8,1,1536]{4,2,3,1,0:T(8,128)(2,1)S(1)}) fusion(bf16[4,8,8,1,1536]{4,2,3,1,0:T(8,128)(2,1)S(1)} %copy-done, bf16[4,11,8,1,1536]{4,2,3,1,0:T(8,128)(2,1)S(1)} %constant_dynamic-update-slice_fusion.3), kind=kLoop, calls=%fused_computation.70 | loop fusion | flops 393215 | bytes 3932160
  33.0 0.0 collective-permute-done.2
  33.0 1.3 %fusion.33 = (bf16[4,8,8,1,1536]{4,2,3,1,0:T(8,128)(2,1)S(1)}, bf16[4,8,8,1,1536]{4,2,3,1,0:T(8,128)(2,1)}, bf16[4,8,8,1,1536]{4,2,3,1,0:T(8,128)(2,1)}) fusion(bf16[4,11,8,1,1536]{4,2,3,1,0:T(8,128)(2,1)S(1)} %constant_dynamic-update-slice_fusion), kind=kLoop, calls=%fused_computation.120 | loop fusion | bytes 4718592 | tf_op jit(solution)/shard_map/slice | solution.py:64
  34.4 0.2 reshape.593
  34.6 2.1 %convolution_bitcast_fusion.6 = f32[4,8,2,4,1,1536]{5,3,2,1,0,4:T(4,128)S(1)} fusion(bf16[4,8,2,4,1536]{4,3,2,1,0:T(4,128)(2,1)S(1)} %reshape.593, f32[4,4]{1,0:T(4,128)} %get-tuple-element.16), kind=kOutput, calls=%fused_computation.6 | convolution fusion | flops 18874368 | bytes 2359360 | tf_op jit(solution)/shard_map/vw,...cwxn->...cvxn/dot_general | solution.py:66
  36.6 0.3 multiply_subtract_fusion.6
  37.0 0.4 pad_maximum_fusion
  37.4 1.7 %stack.50 = f32[4,8,8,1,1536]{4,2,1,0,3:T(8,128)} reshape(f32[4,8,2,4,1,1536]{5,3,2,1,0,4:T(4,128)S(1)} %pad_maximum_fusion) | data formatting | bytes 3145728 | tf_op jit(solution)/shard_map/stack | solution.py:73
  39.1 1.8 %reshape.595 = bf16[4,8,2,4,1536]{4,3,2,1,0:T(4,128)(2,1)S(1)} reshape(bf16[4,8,8,1,1536]{4,2,3,1,0:T(8,128)(2,1)} %get-tuple-element.47) | data formatting | bytes 1572864 | tf_op jit(solution)/shard_map/reshape.29
  40.8 1.1 reshape.594
  41.9 1.4 %convolution_bitcast_fusion.4 = f32[4,8,2,4,1,1536]{5,3,2,1,0,4:T(4,128)S(1)} fusion(bf16[4,8,2,4,1536]{4,3,2,1,0:T(4,128)(2,1)S(1)} %reshape.595, f32[4,4]{1,0:T(4,128)S(1)} %copy-done.17), kind=kOutput, calls=%fused_computation.4 | convolution fusion | flops 18874368 | bytes 2359360 | tf_op jit(solution)/shard_map/vw,...cwxn->...cvxn/dot_general | solution.py:66
  43.3 1.4 %convolution_bitcast_fusion.5 = f32[4,8,2,4,1,1536]{5,3,2,1,0,4:T(4,128)S(1)} fusion(bf16[4,8,2,4,1536]{4,3,2,1,0:T(4,128)(2,1)S(1)} %copy-done.5, f32[4,4]{1,0:T(4,128)S(1)} %copy-done.16), kind=kOutput, calls=%fused_computation.5 | convolution fusion | flops 18874368 | bytes 2359360 | tf_op jit(solution)/shard_map/vw,...cwxn->...cvxn/dot_general | solution.py:66
  44.7 1.8 %multiply_subtract_fusion.4 = (f32[4,8,1,4,1,1536]{5,3,2,1,0,4:T(4,128)S(1)}, f32[4,8,1,4,1,1536]{5,3,2,1,0,4:T(4,128)S(1)}, f32[4,8,1,4,1,1536]{5,3,2,1,0,4:T(4,128)}, f32[4,8,1,4,1,1536]{5,3,2,1,0,4:T(4,128)}) fusion(f32[4,8,2,4,1,1536]{5,3,2,1,0,4:T(4,128)S(1)} %convolution_bitcast_fusion.4, f32[1536]{0:T(1024)S(1)} %get-tuple-element.9, ...), kind=kLoop, calls=%fused_computation.55 | loop fusion | flops 2359296 | bytes 6316032 | tf_op jit(solution)/shard_map/sub | solution.py:74
  46.5 0.4 pad_maximum_fusion.2
  46.9 1.7 %stack.54 = f32[4,8,8,1,1536]{4,2,1,0,3:T(8,128)} reshape(f32[4,8,2,4,1,1536]{5,3,2,1,0,4:T(4,128)S(1)} %pad_maximum_fusion.2) | data formatting | bytes 3145728 | tf_op jit(solution)/shard_map/stack | solution.py:73
  48.6 1.8 %pad_maximum_fusion.1 = f32[4,8,2,4,1,1536]{5,3,2,1,0,4:T(4,128)S(1)} fusion(f32[4,8,1,4,1,1536]{5,3,2,1,0,4:T(4,128)} %get-tuple-element.80, f32[4,8,1,4,1,1536]{5,3,2,1,0,4:T(4,128)} %get-tuple-element.81), kind=kLoop, calls=%fused_computation.21 | loop fusion | flops 393216 | bytes 3145728 | tf_op jit(solution)/shard_map/stack | solution.py:73
  50.4 1.7 %stack.52 = f32[4,8,8,1,1536]{4,2,1,0,3:T(8,128)} reshape(f32[4,8,2,4,1,1536]{5,3,2,1,0,4:T(4,128)S(1)} %pad_maximum_fusion.1) | data formatting | bytes 3145728 | tf_op jit(solution)/shard_map/stack | solution.py:73
  52.0 1.3 %fusion.34 = (bf16[4,8,8,1,1536]{4,2,3,1,0:T(8,128)(2,1)}, bf16[4,8,8,1,1536]{4,2,3,1,0:T(8,128)(2,1)}, bf16[4,8,8,1,1536]{4,2,3,1,0:T(8,128)(2,1)S(1)}) fusion(bf16[4,11,8,1,1536]{4,2,3,1,0:T(8,128)(2,1)S(1)} %get-tuple-element.58), kind=kLoop, calls=%fused_computation.121 | loop fusion | bytes 4718592 | tf_op jit(solution)/shard_map/slice | solution.py:64
  53.4 1.7 %reshape.597 = bf16[4,8,2,4,1536]{4,3,2,1,0:T(4,128)(2,1)S(1)} reshape(bf16[4,8,8,1,1536]{4,2,3,1,0:T(8,128)(2,1)} %get-tuple-element.49) | data formatting | bytes 1572864 | tf_op jit(solution)/shard_map/reshape.43
  55.1 1.4 %convolution_bitcast_fusion.2 = f32[4,8,2,4,1,1536]{5,3,2,1,0,4:T(4,128)S(1)} fusion(bf16[4,8,2,4,1536]{4,3,2,1,0:T(4,128)(2,1)S(1)} %reshape.597, f32[4,4]{1,0:T(4,128)S(1)} %copy-done.15), kind=kOutput, calls=%fused_computation.2 | convolution fusion | flops 18874368 | bytes 2359360 | tf_op jit(solution)/shard_map/vw,...cwxn->...cvxn/dot_general | solution.py:66
  56.5 0.0 copy-done.1
  56.5 1.9 %multiply_subtract_fusion.2 = (f32[4,8,1,4,1,1536]{5,3,2,1,0,4:T(4,128)S(1)}, f32[4,8,1,4,1,1536]{5,3,2,1,0,4:T(4,128)S(1)}, f32[4,8,1,4,1,1536]{5,3,2,1,0,4:T(4,128)}, f32[4,8,1,4,1,1536]{5,3,2,1,0,4:T(4,128)}) fusion(f32[4,8,2,4,1,1536]{5,3,2,1,0,4:T(4,128)S(1)} %convolution_bitcast_fusion.2, f32[1536]{0:T(1024)S(1)} %get-tuple-element.5, ...), kind=kLoop, calls=%fused_computation.51 | loop fusion | flops 2359296 | bytes 6316032 | tf_op jit(solution)/shard_map/sub | solution.py:74
  58.3 0.4 pad_maximum_fusion.4
  58.7 1.7 %stack.58 = f32[4,8,8,1,1536]{4,2,1,0,3:T(8,128)} reshape(f32[4,8,2,4,1,1536]{5,3,2,1,0,4:T(4,128)S(1)} %pad_maximum_fusion.4) | data formatting | bytes 3145728 | tf_op jit(solution)/shard_map/stack | solution.py:73
  60.4 1.9 %reshape.599 = bf16[4,8,2,4,1536]{4,3,2,1,0:T(4,128)(2,1)S(1)} reshape(bf16[4,8,8,1,1536]{4,2,3,1,0:T(8,128)(2,1)} %get-tuple-element.50) | data formatting | bytes 1572864 | tf_op jit(solution)/shard_map/reshape.57
  62.3 0.2 reshape.598
  62.6 1.4 %convolution_bitcast_fusion = f32[4,8,2,4,1,1536]{5,3,2,1,0,4:T(4,128)S(1)} fusion(bf16[4,8,2,4,1536]{4,3,2,1,0:T(4,128)(2,1)S(1)} %reshape.599, f32[4,4]{1,0:T(4,128)S(1)} %copy-done.14), kind=kOutput, calls=%fused_computation | convolution fusion | flops 18874368 | bytes 2359360 | tf_op jit(solution)/shard_map/vw,...cwxn->...cvxn/dot_general | solution.py:66
  63.9 1.4 %convolution_bitcast_fusion.1 = f32[4,8,2,4,1,1536]{5,3,2,1,0,4:T(4,128)S(1)} fusion(bf16[4,8,2,4,1536]{4,3,2,1,0:T(4,128)(2,1)S(1)} %reshape.598, f32[4,4]{1,0:T(4,128)S(1)} %copy-done.13), kind=kOutput, calls=%fused_computation.1 | convolution fusion | flops 18874368 | bytes 2359360 | tf_op jit(solution)/shard_map/vw,...cwxn->...cvxn/dot_general | solution.py:66
  65.3 1.5 %multiply_subtract_fusion = (f32[4,8,1,4,1,1536]{5,3,2,1,0,4:T(4,128)S(1)}, f32[4,8,1,4,1,1536]{5,3,2,1,0,4:T(4,128)S(1)}, f32[4,8,1,4,1,1536]{5,3,2,1,0,4:T(4,128)S(1)}, f32[4,8,1,4,1,1536]{5,3,2,1,0,4:T(4,128)}) fusion(f32[4,8,2,4,1,1536]{5,3,2,1,0,4:T(4,128)S(1)} %convolution_bitcast_fusion, f32[1536]{0:T(1024)S(1)} %get-tuple-element.14, ...), kind=kLoop, calls=%fused_computation.47 | loop fusion | flops 2359296 | bytes 6316032 | tf_op jit(solution)/shard_map/sub | solution.py:74
  66.9 0.4 pad_maximum_fusion.6
  67.2 1.7 %stack.62 = f32[4,8,8,1,1536]{4,2,1,0,3:T(8,128)} reshape(f32[4,8,2,4,1,1536]{5,3,2,1,0,4:T(4,128)S(1)} %pad_maximum_fusion.6) | data formatting | bytes 3145728 | tf_op jit(solution)/shard_map/stack | solution.py:73
  68.9 1.5 %pad_maximum_fusion.5 = f32[4,8,2,4,1,1536]{5,3,2,1,0,4:T(4,128)S(1)} fusion(f32[4,8,1,4,1,1536]{5,3,2,1,0,4:T(4,128)S(1)} %get-tuple-element.76, f32[4,8,1,4,1,1536]{5,3,2,1,0,4:T(4,128)} %get-tuple-element.77), kind=kLoop, calls=%fused_computation.25 | loop fusion | flops 393216 | bytes 3145728 | tf_op jit(solution)/shard_map/stack | solution.py:73
  70.4 1.7 %stack.60 = f32[4,8,8,1,1536]{4,2,1,0,3:T(8,128)} reshape(f32[4,8,2,4,1,1536]{5,3,2,1,0,4:T(4,128)S(1)} %pad_maximum_fusion.5) | data formatting | bytes 3145728 | tf_op jit(solution)/shard_map/stack | solution.py:73
  72.1 1.5 %pad_maximum_fusion.3 = f32[4,8,2,4,1,1536]{5,3,2,1,0,4:T(4,128)S(1)} fusion(f32[4,8,1,4,1,1536]{5,3,2,1,0,4:T(4,128)S(1)} %copy-done.4, f32[4,8,1,4,1,1536]{5,3,2,1,0,4:T(4,128)} %get-tuple-element.79), kind=kLoop, calls=%fused_computation.23 | loop fusion | flops 393216 | bytes 3145728 | tf_op jit(solution)/shard_map/stack | solution.py:73
  73.7 1.7 %stack.56 = f32[4,8,8,1,1536]{4,2,1,0,3:T(8,128)} reshape(f32[4,8,2,4,1,1536]{5,3,2,1,0,4:T(4,128)S(1)} %pad_maximum_fusion.3) | data formatting | bytes 3145728 | tf_op jit(solution)/shard_map/stack | solution.py:73
  75.4 3.3 %slice_multiply_fusion.1 = (f32[4,8,4,1,1536]{4,2,3,1,0:T(4,128)S(1)}, f32[4,8,4,1,1536]{4,2,3,1,0:T(4,128)}) fusion(f32[4,8,8,1,1536]{4,2,3,1,0:T(8,128)} %get-tuple-element.57, f32[8]{0:T(128)} %get-tuple-element.75, f32[8]{0:T(128)} %get-tuple-element.74), kind=kLoop, calls=%fused_computation.45 | loop fusion | flops 393216 | bytes 3145792 | tf_op jit(solution)/shard_map/mul | solution.py:56
  78.8 0.0 collective-permute-done
  78.8 0.0 collective-permute-done.1
  78.8 11.0 %fusion.1 = bf16[4,8,8,1,1536]{4,2,3,1,0:T(8,128)(2,1)} fusion(f32[4,8,4,1,1536]{4,2,3,1,0:T(4,128)} %get-tuple-element.45, f32[4,8,4,1,1536]{4,2,3,1,0:T(4,128)S(1)} %get-tuple-element.44, f32[4,8,8,1,48]{4,2,3,1,0:T(8,128)} %get-tuple-element.68, f32[4,8,8,1,1488]{4,2,3,1,0:T(8,128)} %get-tuple-element.70, f32[4,8,8,1,1488]{4,2,3,1,0:T(8,128)} %get-tuple-element.69, ...), kind=kLoop, calls=%fused_computation.9 | loop fusion | flops 15335424 | bytes 25178336 | tf_op jit(solution)/shard_map/convert_element_type | solution.py:103
  89.8 3.2 %fusion.14 = f32[4,4]{1,0:T(4,128)S(1)} fusion(bf16[4,8,8,1536]{3,2,1,0:T(8,128)(2,1)} %bitcast.161), kind=kOutput, calls=%fused_computation.43 | convolution fusion | flops 3145744 | bytes 786496 | tf_op jit(solution)/shard_map/dot_general | solution.py:113
  93.0 22.8 %psum.14 = f32[4,4]{1,0:T(4,128)S(1)} all-reduce(f32[4,4]{1,0:T(4,128)S(1)} %fusion.14), channel_id=1, replica_groups=mesh['space'=8,'freq'=4] {'space'}, use_global_device_ids=true, to_apply=%region_0.1 | all-reduce | flops 16 | bytes 128 | tf_op jit(solution)/shard_map/psum | solution.py:114
  115.8 6.2 %psum.15 = f32[4,4]{1,0:T(4,128)} all-reduce(f32[4,4]{1,0:T(4,128)S(1)} %psum.14), channel_id=1, replica_groups=mesh['space'=8,'freq'=4] {'freq'}, use_global_device_ids=true, to_apply=%region_1.2 | all-reduce | flops 16 | bytes 128 | tf_op jit(solution)/shard_map/psum | solution.py:115
  (41 shorter events, 0.1 us)
Async XLA Ops:
  0.6 6.8 %copy-start = (bf16[4,8,8,1,1536]{4,2,3,1,0:T(8,128)(2,1)S(1)}, bf16[4,8,8,1,1536]{4,2,3,1,0:T(8,128)(2,1)}, u32[]{:S(2)}) copy-start(bf16[4,8,8,1,1536]{4,2,3,1,0:T(8,128)(2,1)} %param.6) | copy-start | bytes 2359300
  1.8 31.2 %collective-permute-start.2 = (bf16[4,3,8,1,1536]{4,2,3,1,0:T(8,128)(2,1)S(1)}, bf16[4,3,8,1,1536]{4,2,3,1,0:T(8,128)(2,1)S(1)}, u32[]{:S(2)}, u32[]{:S(2)}) collective-permute-start(bf16[4,3,8,1,1536]{4,2,3,1,0:T(8,128)(2,1)S(1)} %get-tuple-element.54), channel_id=1, source_target_pairs={{1,0},{2,1},{3,2},{5,4},{6,5},{7,6},{9,8},{10,9},{11,10},{13,12},{... | collective-permute-start | bytes 884744 | tf_op jit(solution)/shard_map/ppermute | solution.py:29
  3.1 28.4 %collective-permute-start.3 = (bf16[4,3,8,1,1536]{4,2,3,1,0:T(8,128)(2,1)S(1)}, bf16[4,3,8,1,1536]{4,2,3,1,0:T(8,128)(2,1)S(1)}, u32[]{:S(2)}, u32[]{:S(2)}) collective-permute-start(bf16[4,3,8,1,1536]{4,2,3,1,0:T(8,128)(2,1)S(1)} %get-tuple-element.55), channel_id=1, source_target_pairs={{0,1},{1,2},{2,3},{4,5},{5,6},{6,7},{8,9},{9,10},{10,11},{12,13},{... | collective-permute-start | bytes 884744 | tf_op jit(solution)/shard_map/ppermute | solution.py:27
  8.9 69.9 %collective-permute-start = (bf16[4,8,8,1,1536]{4,2,3,1,0:T(8,128)(2,1)}, bf16[4,8,8,1,1536]{4,2,3,1,0:T(8,128)(2,1)}, u32[]{:S(2)}, u32[]{:S(2)}) collective-permute-start(bf16[4,8,8,1,1536]{4,2,3,1,0:T(8,128)(2,1)} %get-tuple-element.52), channel_id=1, source_target_pairs={{0,4},{4,8},{8,12},{12,16},{16,20},{20,24},{24,28},{1,5},{5,9},{9,... | collective-permute-start | bytes 2359304 | tf_op jit(solution)/shard_map/ppermute | solution.py:16
  14.7 64.1 %collective-permute-start.1 = (bf16[4,8,8,1,1536]{4,2,3,1,0:T(8,128)(2,1)}, bf16[4,8,8,1,1536]{4,2,3,1,0:T(8,128)(2,1)}, u32[]{:S(2)}, u32[]{:S(2)}) collective-permute-start(bf16[4,8,8,1,1536]{4,2,3,1,0:T(8,128)(2,1)} %get-tuple-element.53), channel_id=1, source_target_pairs={{4,0},{8,4},{12,8},{16,12},{20,16},{24,20},{28,24},{5,1},{9,5},{13... | collective-permute-start | bytes 2359304 | tf_op jit(solution)/shard_map/ppermute | solution.py:16
  23.1 2.8 %copy-start.10 = (s32[8,7]{1,0:T(8,128)S(1)}, s32[8,7]{1,0:T(8,128)}, u32[]{:S(2)}) copy-start(s32[8,7]{1,0:T(8,128)} %param.11) | copy-start | bytes 676
  23.1 3.6 %copy-start.9 = (f32[7,4,4]{0,2,1:T(4,128)S(1)}, f32[7,4,4]{0,2,1:T(4,128)}, u32[]{:S(2)}) copy-start(f32[7,4,4]{0,2,1:T(4,128)} %param.8) | copy-start | bytes 1348
  23.1 4.3 %copy-start.11 = (f32[7,2,1,1536]{3,2,1,0:T(1,128)S(1)}, f32[7,2,1,1536]{3,2,1,0:T(1,128)}, u32[]{:S(2)}) copy-start(f32[7,2,1,1536]{3,2,1,0:T(1,128)} %param.7) | copy-start | bytes 258052
  39.1 1.8 %copy-start.3 = (bf16[4,8,8,1,1536]{4,2,3,1,0:T(8,128)(2,1)S(1)}, bf16[4,8,8,1,1536]{4,2,3,1,0:T(8,128)(2,1)}, u32[]{:S(2)}) copy-start(bf16[4,8,8,1,1536]{4,2,3,1,0:T(8,128)(2,1)} %get-tuple-element.48) | copy-start | bytes 2359300
  39.1 2.8 %copy-start.17 = (f32[4,4]{1,0:T(4,128)S(1)}, f32[4,4]{1,0:T(4,128)}, u32[]{:S(2)}) copy-start(f32[4,4]{1,0:T(4,128)} %get-tuple-element.19) | copy-start | bytes 196
  41.9 1.4 %copy-start.5 = (bf16[4,8,2,4,1536]{4,3,2,1,0:T(4,128)(2,1)S(1)}, bf16[4,8,2,4,1536]{4,3,2,1,0:T(4,128)(2,1)}, u32[]{:S(2)}) copy-start(bf16[4,8,2,4,1536]{4,3,2,1,0:T(4,128)(2,1)} %reshape.594) | copy-start | bytes 2359300
  41.9 1.4 %copy-start.16 = (f32[4,4]{1,0:T(4,128)S(1)}, f32[4,4]{1,0:T(4,128)}, u32[]{:S(2)}) copy-start(f32[4,4]{1,0:T(4,128)} %get-tuple-element.20) | copy-start | bytes 196
  53.4 1.7 %copy-start.15 = (f32[4,4]{1,0:T(4,128)S(1)}, f32[4,4]{1,0:T(4,128)}, u32[]{:S(2)}) copy-start(f32[4,4]{1,0:T(4,128)} %get-tuple-element.17) | copy-start | bytes 196
  55.1 1.4 %copy-start.1 = (f32[4,8,2,4,1,1536]{5,3,2,1,0,4:T(4,128)S(1)}, f32[4,8,2,4,1,1536]{5,3,2,1,0,4:T(4,128)}, u32[]{:S(2)}) copy-start(f32[4,8,2,4,1,1536]{5,3,2,1,0,4:T(4,128)} %convolution_bitcast_fusion.3) | copy-start | bytes 4718596
  60.4 2.1 %copy-start.14 = (f32[4,4]{1,0:T(4,128)S(1)}, f32[4,4]{1,0:T(4,128)}, u32[]{:S(2)}) copy-start(f32[4,4]{1,0:T(4,128)} %get-tuple-element.21) | copy-start | bytes 196
  62.5 1.4 %copy-start.13 = (f32[4,4]{1,0:T(4,128)S(1)}, f32[4,4]{1,0:T(4,128)}, u32[]{:S(2)}) copy-start(f32[4,4]{1,0:T(4,128)} %get-tuple-element.22) | copy-start | bytes 196
  70.4 1.7 %copy-start.4 = (f32[4,8,1,4,1,1536]{5,3,2,1,0,4:T(4,128)S(1)}, f32[4,8,1,4,1,1536]{5,3,2,1,0,4:T(4,128)}, u32[]{:S(2)}) copy-start(f32[4,8,1,4,1,1536]{5,3,2,1,0,4:T(4,128)} %get-tuple-element.78) | copy-start | bytes 2359300
  75.4 3.4 %copy-start.2 = (f32[4,8,8,1,1536]{4,2,1,0,3:T(8,128)S(1)}, f32[4,8,8,1,1536]{4,2,1,0,3:T(8,128)}, u32[]{:S(2)}) copy-start(f32[4,8,8,1,1536]{4,2,1,0,3:T(8,128)} %stack.50) | copy-start | bytes 4718596
  75.4 3.4 %copy-start.6 = (f32[4,8,8,1,47]{4,2,3,1,0:T(8,128)S(1)}, f32[4,8,8,1,47]{4,2,3,1,0:T(8,128)}, u32[]{:S(2)}) copy-start(f32[4,8,8,1,47]{4,2,3,1,0:T(8,128)} %get-tuple-element.65) | copy-start | bytes 144388
  75.4 3.4 %copy-start.7 = (f32[4,8,8,1,47]{4,2,3,1,0:T(8,128)S(1)}, f32[4,8,8,1,47]{4,2,3,1,0:T(8,128)}, u32[]{:S(2)}) copy-start(f32[4,8,8,1,47]{4,2,3,1,0:T(8,128)} %get-tuple-element.66) | copy-start | bytes 144388
  75.4 3.4 %copy-start.8 = (f32[4,8,8,1,1]{4,2,3,1,0:T(8,128)S(1)}, f32[4,8,8,1,1]{4,2,3,1,0:T(8,128)}, u32[]{:S(2)}) copy-start(f32[4,8,8,1,1]{4,2,3,1,0:T(8,128)} %get-tuple-element.59) | copy-start | bytes 3076
  75.4 3.4 %copy-start.12 = (f32[1536]{0:T(1024)S(1)}, f32[1536]{0:T(1024)}, u32[]{:S(2)}) copy-start(f32[1536]{0:T(1024)} %get-tuple-element.71) | copy-start | bytes 18436
  75.4 3.4 %copy-start.18 = (pred[1536]{0:T(1024)(128)(4,1)S(1)}, pred[1536]{0:T(1024)(128)(4,1)}, u32[]{:S(2)}) copy-start(pred[1536]{0:T(1024)(128)(4,1)} %get-tuple-element.84) | copy-start | bytes 4612
  75.4 3.4 %copy-start.19 = (pred[1536]{0:T(1024)(128)(4,1)S(1)}, pred[1536]{0:T(1024)(128)(4,1)}, u32[]{:S(2)}) copy-start(pred[1536]{0:T(1024)(128)(4,1)} %get-tuple-element.85) | copy-start | bytes 4612
where the time goes:
time: 123 us; the launch traced here: 122 us
  other arithmetic  32.9 us (27%)
  local copies, waits for them, and re-layouts  32.3 us (26%)
  blocking collectives  29 us (24%)
  matrix products  14.7 us (12%)
  starting transfers between devices  11.4 us (9%)
  between operations  1.65 us (1%)
    psum x1, blocking collectives, local(): gram_matrix = lax.psum(partial_value, 'space')  22.8 us
    another operation x7, local copies, waits for them, and re-layouts, coupling(): jnp.stack([base_re * mix_re - base_im * mix_im, base_re * mix_im + base_i...  11.9 us
    dot_general x7, matrix products, coupling(): jnp.einsum('vw,...cwxn->...cvxn', mixing[j], halves, precision=lax.Precis...  11.5 us
    convert_element_type x1, other arithmetic, local(): response = result.astype(jnp.bfloat16)  11 us
    ppermute x2, starting transfers between devices, passed_along(): return lax.ppermute(value, axis, pairs)  7.08 us
    another operation x7, local copies, waits for them, and re-layouts  6.95 us
    another operation x7, other arithmetic, coupling(): jnp.stack([base_re * mix_re - base_im * mix_im, base_re * mix_im + base_i...  6.26 us
    psum x1, blocking collectives, local(): gram_matrix = lax.psum(gram_matrix, 'freq')  6.22 us
  transfers between devices with their start and end apart: 4, of which 0 were waited for; matrix products, arithmetic and copies ran while one was open for 53% of the time, Pallas kernels for 0%

commit v1 on v0

--- a/solution.py
+++ b/solution.py
@@ -111,7 +111,11 @@
         * forcing.shape[4]
     )
     partial_value = jnp.dot(flattened, flattened.T, preferred_element_type=jnp.float32) / cells_all
-    gram_matrix = lax.psum(partial_value, "space")
+    gram_matrix = partial_value
+    for hop in (1, 2, 4):
+        gram_matrix = gram_matrix + lax.ppermute(
+            gram_matrix, "space", [(dev, dev ^ hop) for dev in range(8)]
+        )
     gram_matrix = lax.psum(gram_matrix, "freq")
     return (response, gram_matrix)
 

time: 123 us -> 112 us (0.911)
  blocking collectives: 29 us -> 6.21 us
  starting transfers between devices: 11.4 us -> 19.2 us
  waiting for transfers between devices: 0.01 us -> 4.7 us
    psum x1 -> x0, blocking collectives: 22.8 us -> none  [local(): gram_matrix = lax.psum(partial_value, 'space')]
    ppermute x0 -> x3, starting transfers between devices: none -> 7.79 us  [local(): lax.ppermute(gram_matrix, 'space', [(dev, dev ^ hop) for dev in range(8)])]
    ppermute x0 -> x3, waiting for transfers between devices: none -> 4.69 us  [local(): lax.ppermute(gram_matrix, 'space', [(dev, dev ^ hop) for dev in range(8)])]
  transfers between devices with their start and end apart: 4 -> 7, of which waited for: 0 -> 3; matrix products, arithmetic and copies ran while one was open for 53% -> 58% of each run, Pallas kernels for 0% -> 0%
where the time goes in v1:
time: 112 us
  other arithmetic  32.9 us (29%)
  local copies, waits for them, and re-layouts  32.3 us (29%)
  starting transfers between devices  19.2 us (17%)
  matrix products  14.7 us (13%)
  blocking collectives  6.21 us (6%)
  waiting for transfers between devices  4.7 us (4%)
  between operations  1.65 us (1%)
    another operation x7, local copies, waits for them, and re-layouts, coupling(): jnp.stack([base_re * mix_re - base_im * mix_im, base_re * mix_im + base_i...  11.9 us
    dot_general x7, matrix products, coupling(): jnp.einsum('vw,...cwxn->...cvxn', mixing[j], halves, precision=lax.Precis...  11.5 us
    convert_element_type x1, other arithmetic, local(): response = result.astype(jnp.bfloat16)  11 us
    ppermute x3, starting transfers between devices, local(): lax.ppermute(gram_matrix, 'space', [(dev, dev ^ hop) for dev in range(8)])  7.79 us
    ppermute x2, starting transfers between devices, passed_along(): return lax.ppermute(value, axis, pairs)  7.08 us
    another operation x7, local copies, waits for them, and re-layouts  6.95 us
    another operation x7, other arithmetic, coupling(): jnp.stack([base_re * mix_re - base_im * mix_im, base_re * mix_im + base_i...  6.26 us
    psum x1, blocking collectives, local(): gram_matrix = lax.psum(gram_matrix, 'freq')  6.21 us
  transfers between devices with their start and end apart: 7, of which 3 were waited for; matrix products, arithmetic and copies ran while one was open for 58% of the time, Pallas kernels for 0%

profile of v1, /device:TPU:0, one launch (start us, length us, event | category | flops | bytes accessed | tf_op | source)
XLA Modules:
  0.0 111.7 jit_solution(11470733273986577585)
XLA Ops:
  0.6 1.2 %fusion.35 = (bf16[4,3,8,1,1536]{4,2,3,1,0:T(8,128)(2,1)S(1)}, bf16[4,3,8,1,1536]{4,2,3,1,0:T(8,128)(2,1)S(1)}) fusion(bf16[4,8,8,1,1536]{4,2,3,1,0:T(8,128)(2,1)} %param.6), kind=kLoop, calls=%fused_computation.122 | loop fusion | bytes 1179648 | tf_op jit(solution)/shard_map/slice | solution.py:23
  1.8 1.3 %collective-permute-start.2 = (bf16[4,3,8,1,1536]{4,2,3,1,0:T(8,128)(2,1)S(1)}, bf16[4,3,8,1,1536]{4,2,3,1,0:T(8,128)(2,1)S(1)}, u32[]{:S(2)}, u32[]{:S(2)}) collective-permute-start(bf16[4,3,8,1,1536]{4,2,3,1,0:T(8,128)(2,1)S(1)} %get-tuple-element.54), channel_id=1, source_target_pairs={{1,0},{2,1},{3,2},{5,4},{6,5},{7,6},{9,8},{10,9},{11,10},{13,12},{... | collective-permute-start | bytes 884744 | tf_op jit(solution)/shard_map/ppermute | solution.py:29
  3.1 3.0 %collective-permute-start.3 = (bf16[4,3,8,1,1536]{4,2,3,1,0:T(8,128)(2,1)S(1)}, bf16[4,3,8,1,1536]{4,2,3,1,0:T(8,128)(2,1)S(1)}, u32[]{:S(2)}, u32[]{:S(2)}) collective-permute-start(bf16[4,3,8,1,1536]{4,2,3,1,0:T(8,128)(2,1)S(1)} %get-tuple-element.55), channel_id=1, source_target_pairs={{0,1},{1,2},{2,3},{4,5},{5,6},{6,7},{8,9},{9,10},{10,11},{12,13},{... | collective-permute-start | bytes 884744 | tf_op jit(solution)/shard_map/ppermute | solution.py:27
  6.2 1.3 %add_multiply_fusion = (f32[1536]{0:T(1024)}, f32[1536]{0:T(1024)S(1)}, f32[1536]{0:T(1024)S(1)}) fusion(f32[1536]{0:T(1024)} %param.9), kind=kLoop, calls=%fused_computation.78 | loop fusion | flops 7680 | bytes 24576 | tf_op jit(solution)/shard_map/add | solution.py:49
  7.5 1.4 %multiply_convert_fusion.1 = (bf16[4,8,8,1,1536]{4,2,3,1,0:T(8,128)(2,1)}, bf16[4,8,8,1,1536]{4,2,3,1,0:T(8,128)(2,1)}) fusion(bf16[4,8,8,1,1536]{4,2,3,1,0:T(8,128)(2,1)S(1)} %copy-done, f32[1536]{0:T(1024)S(1)} %get-tuple-element.73, f32[1536]{0:T(1024)S(1)} %get-tuple-element.72), kind=kLoop, calls=%fused_computation.41 | loop fusion | flops 1966080 | bytes 2371584 | tf_op jit(solution)/shard_map/convert_element_type | solution.py:92
  8.9 5.8 %collective-permute-start = (bf16[4,8,8,1,1536]{4,2,3,1,0:T(8,128)(2,1)}, bf16[4,8,8,1,1536]{4,2,3,1,0:T(8,128)(2,1)}, u32[]{:S(2)}, u32[]{:S(2)}) collective-permute-start(bf16[4,8,8,1,1536]{4,2,3,1,0:T(8,128)(2,1)} %get-tuple-element.52), channel_id=1, source_target_pairs={{0,4},{4,8},{8,12},{12,16},{16,20},{20,24},{24,28},{1,5},{5,9},{9,... | collective-permute-start | bytes 2359304 | tf_op jit(solution)/shard_map/ppermute | solution.py:16
  14.7 1.3 %collective-permute-start.1 = (bf16[4,8,8,1,1536]{4,2,3,1,0:T(8,128)(2,1)}, bf16[4,8,8,1,1536]{4,2,3,1,0:T(8,128)(2,1)}, u32[]{:S(2)}, u32[]{:S(2)}) collective-permute-start(bf16[4,8,8,1,1536]{4,2,3,1,0:T(8,128)(2,1)} %get-tuple-element.53), channel_id=1, source_target_pairs={{4,0},{8,4},{12,8},{16,12},{20,16},{24,20},{28,24},{5,1},{9,5},{13... | collective-permute-start | bytes 2359304 | tf_op jit(solution)/shard_map/ppermute | solution.py:16
  16.0 0.6 broadcast_compare_fusion
  16.6 0.6 fusion.22
  17.2 0.7 fusion.39
  17.9 0.7 fusion.36
  18.7 0.2 reshape.596
  18.9 2.1 %fusion.38 = (f32[4,8,8,1,1489]{4,2,3,1,0:T(8,128)}, f32[4,8,8,1,1489]{4,2,3,1,0:T(8,128)}) fusion(bf16[4,8,8,1,1536]{4,2,3,1,0:T(8,128)(2,1)S(1)} %copy-done), kind=kLoop, calls=%fused_computation.125 | loop fusion | bytes 6098944 | tf_op jit(solution)/shard_map/jit(_roll_static)/slice | solution.py:42
  21.0 2.1 %fusion.41 = (f32[4,8,8,1,1488]{4,2,3,1,0:T(8,128)}, f32[4,8,8,1,1488]{4,2,3,1,0:T(8,128)}) fusion(bf16[4,8,8,1,1536]{4,2,3,1,0:T(8,128)(2,1)S(1)} %copy-done), kind=kLoop, calls=%fused_computation.128 | loop fusion | bytes 6094848 | tf_op jit(solution)/shard_map/jit(_roll_static)/slice | solution.py:44
  23.1 2.1 %fusion.37 = (f32[4,8,8,1,1535]{4,2,3,1,0:T(8,128)}, f32[4,8,8,1,1535]{4,2,3,1,0:T(8,128)}) fusion(bf16[4,8,8,1,1536]{4,2,3,1,0:T(8,128)(2,1)S(1)} %copy-done), kind=kLoop, calls=%fused_computation.124 | loop fusion | bytes 6287360 | tf_op jit(solution)/shard_map/jit(_roll_static)/slice | solution.py:42
  25.8 0.8 convert_reduce_fusion.6
  26.6 0.8 slice_reduce_fusion.6
  27.4 0.2 slice_reduce_fusion.20
  27.6 2.6 %convolution_bitcast_fusion.3 = f32[4,8,2,4,1,1536]{5,3,2,1,0,4:T(4,128)} fusion(bf16[4,8,2,4,1536]{4,3,2,1,0:T(4,128)(2,1)S(1)} %reshape.596, f32[4,4]{1,0:T(4,128)S(1)} %get-tuple-element.18), kind=kOutput, calls=%fused_computation.3 | convolution fusion | flops 18874368 | bytes 2359360 | tf_op jit(solution)/shard_map/vw,...cwxn->...cvxn/dot_general | solution.py:66
  30.2 0.6 convert_multiply_fusion
  30.8 0.7 fusion.40
  31.6 1.5 %constant_dynamic-update-slice_fusion.1 = (bf16[4,11,8,1,1536]{4,2,3,1,0:T(8,128)(2,1)S(1)}, f32[4,8,8,1,1536]{4,2,3,1,0:T(8,128)}, bf16[4,11,8,1,1536]{4,2,3,1,0:T(8,128)(2,1)S(1)}) fusion(bf16[4,8,8,1,1536]{4,2,3,1,0:T(8,128)(2,1)S(1)} %copy-done, bf16[4,11,8,1,1536]{4,2,3,1,0:T(8,128)(2,1)S(1)} %constant_dynamic-update-slice_fusion.3), kind=kLoop, calls=%fused_computation.70 | loop fusion | flops 393215 | bytes 3932160
  33.0 1.3 %fusion.33 = (bf16[4,8,8,1,1536]{4,2,3,1,0:T(8,128)(2,1)S(1)}, bf16[4,8,8,1,1536]{4,2,3,1,0:T(8,128)(2,1)}, bf16[4,8,8,1,1536]{4,2,3,1,0:T(8,128)(2,1)}) fusion(bf16[4,11,8,1,1536]{4,2,3,1,0:T(8,128)(2,1)S(1)} %constant_dynamic-update-slice_fusion), kind=kLoop, calls=%fused_computation.120 | loop fusion | bytes 4718592 | tf_op jit(solution)/shard_map/slice | solution.py:64
  34.4 0.2 reshape.593
  34.6 2.1 %convolution_bitcast_fusion.6 = f32[4,8,2,4,1,1536]{5,3,2,1,0,4:T(4,128)S(1)} fusion(bf16[4,8,2,4,1536]{4,3,2,1,0:T(4,128)(2,1)S(1)} %reshape.593, f32[4,4]{1,0:T(4,128)} %get-tuple-element.16), kind=kOutput, calls=%fused_computation.6 | convolution fusion | flops 18874368 | bytes 2359360 | tf_op jit(solution)/shard_map/vw,...cwxn->...cvxn/dot_general | solution.py:66
  36.6 0.3 multiply_subtract_fusion.6
  37.0 0.4 pad_maximum_fusion
  37.4 1.7 %stack.50 = f32[4,8,8,1,1536]{4,2,1,0,3:T(8,128)} reshape(f32[4,8,2,4,1,1536]{5,3,2,1,0,4:T(4,128)S(1)} %pad_maximum_fusion) | data formatting | bytes 3145728 | tf_op jit(solution)/shard_map/stack | solution.py:73
  39.1 1.8 %reshape.595 = bf16[4,8,2,4,1536]{4,3,2,1,0:T(4,128)(2,1)S(1)} reshape(bf16[4,8,8,1,1536]{4,2,3,1,0:T(8,128)(2,1)} %get-tuple-element.47) | data formatting | bytes 1572864 | tf_op jit(solution)/shard_map/reshape.29
  40.8 1.1 reshape.594
  41.9 1.4 %convolution_bitcast_fusion.4 = f32[4,8,2,4,1,1536]{5,3,2,1,0,4:T(4,128)S(1)} fusion(bf16[4,8,2,4,1536]{4,3,2,1,0:T(4,128)(2,1)S(1)} %reshape.595, f32[4,4]{1,0:T(4,128)S(1)} %copy-done.17), kind=kOutput, calls=%fused_computation.4 | convolution fusion | flops 18874368 | bytes 2359360 | tf_op jit(solution)/shard_map/vw,...cwxn->...cvxn/dot_general | solution.py:66
  43.3 1.4 %convolution_bitcast_fusion.5 = f32[4,8,2,4,1,1536]{5,3,2,1,0,4:T(4,128)S(1)} fusion(bf16[4,8,2,4,1536]{4,3,2,1,0:T(4,128)(2,1)S(1)} %copy-done.5, f32[4,4]{1,0:T(4,128)S(1)} %copy-done.16), kind=kOutput, calls=%fused_computation.5 | convolution fusion | flops 18874368 | bytes 2359360 | tf_op jit(solution)/shard_map/vw,...cwxn->...cvxn/dot_general | solution.py:66
  44.7 1.8 %multiply_subtract_fusion.4 = (f32[4,8,1,4,1,1536]{5,3,2,1,0,4:T(4,128)S(1)}, f32[4,8,1,4,1,1536]{5,3,2,1,0,4:T(4,128)S(1)}, f32[4,8,1,4,1,1536]{5,3,2,1,0,4:T(4,128)}, f32[4,8,1,4,1,1536]{5,3,2,1,0,4:T(4,128)}) fusion(f32[4,8,2,4,1,1536]{5,3,2,1,0,4:T(4,128)S(1)} %convolution_bitcast_fusion.4, f32[1536]{0:T(1024)S(1)} %get-tuple-element.9, ...), kind=kLoop, calls=%fused_computation.55 | loop fusion | flops 2359296 | bytes 6316032 | tf_op jit(solution)/shard_map/sub | solution.py:74
  46.5 0.4 pad_maximum_fusion.2
  46.9 1.7 %stack.54 = f32[4,8,8,1,1536]{4,2,1,0,3:T(8,128)} reshape(f32[4,8,2,4,1,1536]{5,3,2,1,0,4:T(4,128)S(1)} %pad_maximum_fusion.2) | data formatting | bytes 3145728 | tf_op jit(solution)/shard_map/stack | solution.py:73
  48.6 1.8 %pad_maximum_fusion.1 = f32[4,8,2,4,1,1536]{5,3,2,1,0,4:T(4,128)S(1)} fusion(f32[4,8,1,4,1,1536]{5,3,2,1,0,4:T(4,128)} %get-tuple-element.80, f32[4,8,1,4,1,1536]{5,3,2,1,0,4:T(4,128)} %get-tuple-element.81), kind=kLoop, calls=%fused_computation.21 | loop fusion | flops 393216 | bytes 3145728 | tf_op jit(solution)/shard_map/stack | solution.py:73
  50.4 1.7 %stack.52 = f32[4,8,8,1,1536]{4,2,1,0,3:T(8,128)} reshape(f32[4,8,2,4,1,1536]{5,3,2,1,0,4:T(4,128)S(1)} %pad_maximum_fusion.1) | data formatting | bytes 3145728 | tf_op jit(solution)/shard_map/stack | solution.py:73
  52.0 1.3 %fusion.34 = (bf16[4,8,8,1,1536]{4,2,3,1,0:T(8,128)(2,1)}, bf16[4,8,8,1,1536]{4,2,3,1,0:T(8,128)(2,1)}, bf16[4,8,8,1,1536]{4,2,3,1,0:T(8,128)(2,1)S(1)}) fusion(bf16[4,11,8,1,1536]{4,2,3,1,0:T(8,128)(2,1)S(1)} %get-tuple-element.58), kind=kLoop, calls=%fused_computation.121 | loop fusion | bytes 4718592 | tf_op jit(solution)/shard_map/slice | solution.py:64
  53.4 1.7 %reshape.597 = bf16[4,8,2,4,1536]{4,3,2,1,0:T(4,128)(2,1)S(1)} reshape(bf16[4,8,8,1,1536]{4,2,3,1,0:T(8,128)(2,1)} %get-tuple-element.49) | data formatting | bytes 1572864 | tf_op jit(solution)/shard_map/reshape.43
  55.1 1.4 %convolution_bitcast_fusion.2 = f32[4,8,2,4,1,1536]{5,3,2,1,0,4:T(4,128)S(1)} fusion(bf16[4,8,2,4,1536]{4,3,2,1,0:T(4,128)(2,1)S(1)} %reshape.597, f32[4,4]{1,0:T(4,128)S(1)} %copy-done.15), kind=kOutput, calls=%fused_computation.2 | convolution fusion | flops 18874368 | bytes 2359360 | tf_op jit(solution)/shard_map/vw,...cwxn->...cvxn/dot_general | solution.py:66
  56.5 1.9 %multiply_subtract_fusion.2 = (f32[4,8,1,4,1,1536]{5,3,2,1,0,4:T(4,128)S(1)}, f32[4,8,1,4,1,1536]{5,3,2,1,0,4:T(4,128)S(1)}, f32[4,8,1,4,1,1536]{5,3,2,1,0,4:T(4,128)}, f32[4,8,1,4,1,1536]{5,3,2,1,0,4:T(4,128)}) fusion(f32[4,8,2,4,1,1536]{5,3,2,1,0,4:T(4,128)S(1)} %convolution_bitcast_fusion.2, f32[1536]{0:T(1024)S(1)} %get-tuple-element.5, ...), kind=kLoop, calls=%fused_computation.51 | loop fusion | flops 2359296 | bytes 6316032 | tf_op jit(solution)/shard_map/sub | solution.py:74
  58.3 0.4 pad_maximum_fusion.4
  58.7 1.7 %stack.58 = f32[4,8,8,1,1536]{4,2,1,0,3:T(8,128)} reshape(f32[4,8,2,4,1,1536]{5,3,2,1,0,4:T(4,128)S(1)} %pad_maximum_fusion.4) | data formatting | bytes 3145728 | tf_op jit(solution)/shard_map/stack | solution.py:73
  60.4 1.9 %reshape.599 = bf16[4,8,2,4,1536]{4,3,2,1,0:T(4,128)(2,1)S(1)} reshape(bf16[4,8,8,1,1536]{4,2,3,1,0:T(8,128)(2,1)} %get-tuple-element.50) | data formatting | bytes 1572864 | tf_op jit(solution)/shard_map/reshape.57
  62.3 0.2 reshape.598
  62.6 1.4 %convolution_bitcast_fusion = f32[4,8,2,4,1,1536]{5,3,2,1,0,4:T(4,128)S(1)} fusion(bf16[4,8,2,4,1536]{4,3,2,1,0:T(4,128)(2,1)S(1)} %reshape.599, f32[4,4]{1,0:T(4,128)S(1)} %copy-done.14), kind=kOutput, calls=%fused_computation | convolution fusion | flops 18874368 | bytes 2359360 | tf_op jit(solution)/shard_map/vw,...cwxn->...cvxn/dot_general | solution.py:66
  63.9 1.4 %convolution_bitcast_fusion.1 = f32[4,8,2,4,1,1536]{5,3,2,1,0,4:T(4,128)S(1)} fusion(bf16[4,8,2,4,1536]{4,3,2,1,0:T(4,128)(2,1)S(1)} %reshape.598, f32[4,4]{1,0:T(4,128)S(1)} %copy-done.13), kind=kOutput, calls=%fused_computation.1 | convolution fusion | flops 18874368 | bytes 2359360 | tf_op jit(solution)/shard_map/vw,...cwxn->...cvxn/dot_general | solution.py:66
  65.3 1.5 %multiply_subtract_fusion = (f32[4,8,1,4,1,1536]{5,3,2,1,0,4:T(4,128)S(1)}, f32[4,8,1,4,1,1536]{5,3,2,1,0,4:T(4,128)S(1)}, f32[4,8,1,4,1,1536]{5,3,2,1,0,4:T(4,128)S(1)}, f32[4,8,1,4,1,1536]{5,3,2,1,0,4:T(4,128)}) fusion(f32[4,8,2,4,1,1536]{5,3,2,1,0,4:T(4,128)S(1)} %convolution_bitcast_fusion, f32[1536]{0:T(1024)S(1)} %get-tuple-element.14, ...), kind=kLoop, calls=%fused_computation.47 | loop fusion | flops 2359296 | bytes 6316032 | tf_op jit(solution)/shard_map/sub | solution.py:74
  66.9 0.4 pad_maximum_fusion.6
  67.2 1.7 %stack.62 = f32[4,8,8,1,1536]{4,2,1,0,3:T(8,128)} reshape(f32[4,8,2,4,1,1536]{5,3,2,1,0,4:T(4,128)S(1)} %pad_maximum_fusion.6) | data formatting | bytes 3145728 | tf_op jit(solution)/shard_map/stack | solution.py:73
  68.9 1.5 %pad_maximum_fusion.5 = f32[4,8,2,4,1,1536]{5,3,2,1,0,4:T(4,128)S(1)} fusion(f32[4,8,1,4,1,1536]{5,3,2,1,0,4:T(4,128)S(1)} %get-tuple-element.76, f32[4,8,1,4,1,1536]{5,3,2,1,0,4:T(4,128)} %get-tuple-element.77), kind=kLoop, calls=%fused_computation.25 | loop fusion | flops 393216 | bytes 3145728 | tf_op jit(solution)/shard_map/stack | solution.py:73
  70.4 1.7 %stack.60 = f32[4,8,8,1,1536]{4,2,1,0,3:T(8,128)} reshape(f32[4,8,2,4,1,1536]{5,3,2,1,0,4:T(4,128)S(1)} %pad_maximum_fusion.5) | data formatting | bytes 3145728 | tf_op jit(solution)/shard_map/stack | solution.py:73
  72.1 1.5 %pad_maximum_fusion.3 = f32[4,8,2,4,1,1536]{5,3,2,1,0,4:T(4,128)S(1)} fusion(f32[4,8,1,4,1,1536]{5,3,2,1,0,4:T(4,128)S(1)} %copy-done.4, f32[4,8,1,4,1,1536]{5,3,2,1,0,4:T(4,128)} %get-tuple-element.79), kind=kLoop, calls=%fused_computation.23 | loop fusion | flops 393216 | bytes 3145728 | tf_op jit(solution)/shard_map/stack | solution.py:73
  73.7 1.7 %stack.56 = f32[4,8,8,1,1536]{4,2,1,0,3:T(8,128)} reshape(f32[4,8,2,4,1,1536]{5,3,2,1,0,4:T(4,128)S(1)} %pad_maximum_fusion.3) | data formatting | bytes 3145728 | tf_op jit(solution)/shard_map/stack | solution.py:73
  75.4 3.3 %slice_multiply_fusion.1 = (f32[4,8,4,1,1536]{4,2,3,1,0:T(4,128)S(1)}, f32[4,8,4,1,1536]{4,2,3,1,0:T(4,128)}) fusion(f32[4,8,8,1,1536]{4,2,3,1,0:T(8,128)} %get-tuple-element.57, f32[8]{0:T(128)} %get-tuple-element.75, f32[8]{0:T(128)} %get-tuple-element.74), kind=kLoop, calls=%fused_computation.45 | loop fusion | flops 393216 | bytes 3145792 | tf_op jit(solution)/shard_map/mul | solution.py:56
  78.8 11.0 %fusion.1 = bf16[4,8,8,1,1536]{4,2,3,1,0:T(8,128)(2,1)} fusion(f32[4,8,4,1,1536]{4,2,3,1,0:T(4,128)} %get-tuple-element.45, f32[4,8,4,1,1536]{4,2,3,1,0:T(4,128)S(1)} %get-tuple-element.44, f32[4,8,8,1,48]{4,2,3,1,0:T(8,128)} %get-tuple-element.68, f32[4,8,8,1,1488]{4,2,3,1,0:T(8,128)} %get-tuple-element.70, f32[4,8,8,1,1488]{4,2,3,1,0:T(8,128)} %get-tuple-element.69, ...), kind=kLoop, calls=%fused_computation.9 | loop fusion | flops 15335424 | bytes 25178336 | tf_op jit(solution)/shard_map/convert_element_type | solution.py:103
  89.8 3.2 %fusion.14 = f32[4,4]{1,0:T(4,128)S(1)} fusion(bf16[4,8,8,1536]{3,2,1,0:T(8,128)(2,1)} %bitcast.161), kind=kOutput, calls=%fused_computation.43 | convolution fusion | flops 3145744 | bytes 786496 | tf_op jit(solution)/shard_map/dot_general | solution.py:113
  93.0 2.7 %collective-permute-start.4 = (f32[4,4]{1,0:T(4,128)S(1)}, f32[4,4]{1,0:T(4,128)S(1)}, u32[]{:S(2)}, u32[]{:S(2)}) collective-permute-start(f32[4,4]{1,0:T(4,128)S(1)} %fusion.14), channel_id=1, source_target_pairs={{0,4},{4,0},{8,12},{12,8},{16,20},{20,16},{24,28},{28,24},{1,5},{5... | collective-permute-start | bytes 200 | tf_op jit(solution)/shard_map/ppermute | solution.py:116
  95.7 1.6 %collective-permute-done.4 = f32[4,4]{1,0:T(4,128)S(1)} collective-permute-done((f32[4,4]{1,0:T(4,128)S(1)}, f32[4,4]{1,0:T(4,128)S(1)}, u32[]{:S(2)}, u32[]{:S(2)}) %collective-permute-start.4) | collective-permute-done | bytes 96 | tf_op jit(solution)/shard_map/ppermute | solution.py:116
  97.2 2.1 %collective-permute-start.5 = (f32[4,4]{1,0:T(4,128)S(1)}, f32[4,4]{1,0:T(4,128)S(1)}, u32[]{:S(2)}, u32[]{:S(2)}) collective-permute-start(f32[4,4]{1,0:T(4,128)S(1)} %add.228), channel_id=1, source_target_pairs={{0,8},{4,12},{8,0},{12,4},{16,24},{20,28},{24,16},{28,20},{1,9},{5... | collective-permute-start | bytes 200 | tf_op jit(solution)/shard_map/ppermute | solution.py:116
  99.3 1.6 %collective-permute-done.5 = f32[4,4]{1,0:T(4,128)S(1)} collective-permute-done((f32[4,4]{1,0:T(4,128)S(1)}, f32[4,4]{1,0:T(4,128)S(1)}, u32[]{:S(2)}, u32[]{:S(2)}) %collective-permute-start.5) | collective-permute-done | bytes 96 | tf_op jit(solution)/shard_map/ppermute | solution.py:116
  100.9 3.0 %collective-permute-start.6 = (f32[4,4]{1,0:T(4,128)S(1)}, f32[4,4]{1,0:T(4,128)S(1)}, u32[]{:S(2)}, u32[]{:S(2)}) collective-permute-start(f32[4,4]{1,0:T(4,128)S(1)} %add.229), channel_id=1, source_target_pairs={{0,16},{4,20},{8,24},{12,28},{16,0},{20,4},{24,8},{28,12},{1,17},{... | collective-permute-start | bytes 200 | tf_op jit(solution)/shard_map/ppermute | solution.py:116
  103.9 1.6 %collective-permute-done.6 = f32[4,4]{1,0:T(4,128)S(1)} collective-permute-done((f32[4,4]{1,0:T(4,128)S(1)}, f32[4,4]{1,0:T(4,128)S(1)}, u32[]{:S(2)}, u32[]{:S(2)}) %collective-permute-start.6) | collective-permute-done | bytes 96 | tf_op jit(solution)/shard_map/ppermute | solution.py:116
  105.5 6.2 %psum.7 = f32[4,4]{1,0:T(4,128)} all-reduce(f32[4,4]{1,0:T(4,128)S(1)} %add.230), channel_id=1, replica_groups=mesh['space'=8,'freq'=4] {'freq'}, use_global_device_ids=true, to_apply=%region_0.1 | all-reduce | flops 16 | bytes 128 | tf_op jit(solution)/shard_map/psum | solution.py:119
  (49 shorter events, 0.1 us)
Async XLA Ops:
  0.6 6.8 %copy-start = (bf16[4,8,8,1,1536]{4,2,3,1,0:T(8,128)(2,1)S(1)}, bf16[4,8,8,1,1536]{4,2,3,1,0:T(8,128)(2,1)}, u32[]{:S(2)}) copy-start(bf16[4,8,8,1,1536]{4,2,3,1,0:T(8,128)(2,1)} %param.6) | copy-start | bytes 2359300
  1.8 31.2 %collective-permute-start.2 = (bf16[4,3,8,1,1536]{4,2,3,1,0:T(8,128)(2,1)S(1)}, bf16[4,3,8,1,1536]{4,2,3,1,0:T(8,128)(2,1)S(1)}, u32[]{:S(2)}, u32[]{:S(2)}) collective-permute-start(bf16[4,3,8,1,1536]{4,2,3,1,0:T(8,128)(2,1)S(1)} %get-tuple-element.54), channel_id=1, source_target_pairs={{1,0},{2,1},{3,2},{5,4},{6,5},{7,6},{9,8},{10,9},{11,10},{13,12},{... | collective-permute-start | bytes 884744 | tf_op jit(solution)/shard_map/ppermute | solution.py:29
  3.1 28.4 %collective-permute-start.3 = (bf16[4,3,8,1,1536]{4,2,3,1,0:T(8,128)(2,1)S(1)}, bf16[4,3,8,1,1536]{4,2,3,1,0:T(8,128)(2,1)S(1)}, u32[]{:S(2)}, u32[]{:S(2)}) collective-permute-start(bf16[4,3,8,1,1536]{4,2,3,1,0:T(8,128)(2,1)S(1)} %get-tuple-element.55), channel_id=1, source_target_pairs={{0,1},{1,2},{2,3},{4,5},{5,6},{6,7},{8,9},{9,10},{10,11},{12,13},{... | collective-permute-start | bytes 884744 | tf_op jit(solution)/shard_map/ppermute | solution.py:27
  8.9 69.9 %collective-permute-start = (bf16[4,8,8,1,1536]{4,2,3,1,0:T(8,128)(2,1)}, bf16[4,8,8,1,1536]{4,2,3,1,0:T(8,128)(2,1)}, u32[]{:S(2)}, u32[]{:S(2)}) collective-permute-start(bf16[4,8,8,1,1536]{4,2,3,1,0:T(8,128)(2,1)} %get-tuple-element.52), channel_id=1, source_target_pairs={{0,4},{4,8},{8,12},{12,16},{16,20},{20,24},{24,28},{1,5},{5,9},{9,... | collective-permute-start | bytes 2359304 | tf_op jit(solution)/shard_map/ppermute | solution.py:16
  14.7 64.1 %collective-permute-start.1 = (bf16[4,8,8,1,1536]{4,2,3,1,0:T(8,128)(2,1)}, bf16[4,8,8,1,1536]{4,2,3,1,0:T(8,128)(2,1)}, u32[]{:S(2)}, u32[]{:S(2)}) collective-permute-start(bf16[4,8,8,1,1536]{4,2,3,1,0:T(8,128)(2,1)} %get-tuple-element.53), channel_id=1, source_target_pairs={{4,0},{8,4},{12,8},{16,12},{20,16},{24,20},{28,24},{5,1},{9,5},{13... | collective-permute-start | bytes 2359304 | tf_op jit(solution)/shard_map/ppermute | solution.py:16
  23.1 2.8 %copy-start.10 = (s32[8,7]{1,0:T(8,128)S(1)}, s32[8,7]{1,0:T(8,128)}, u32[]{:S(2)}) copy-start(s32[8,7]{1,0:T(8,128)} %param.11) | copy-start | bytes 676
  23.1 3.6 %copy-start.9 = (f32[7,4,4]{0,2,1:T(4,128)S(1)}, f32[7,4,4]{0,2,1:T(4,128)}, u32[]{:S(2)}) copy-start(f32[7,4,4]{0,2,1:T(4,128)} %param.8) | copy-start | bytes 1348
  23.1 4.3 %copy-start.11 = (f32[7,2,1,1536]{3,2,1,0:T(1,128)S(1)}, f32[7,2,1,1536]{3,2,1,0:T(1,128)}, u32[]{:S(2)}) copy-start(f32[7,2,1,1536]{3,2,1,0:T(1,128)} %param.7) | copy-start | bytes 258052
  39.1 1.8 %copy-start.3 = (bf16[4,8,8,1,1536]{4,2,3,1,0:T(8,128)(2,1)S(1)}, bf16[4,8,8,1,1536]{4,2,3,1,0:T(8,128)(2,1)}, u32[]{:S(2)}) copy-start(bf16[4,8,8,1,1536]{4,2,3,1,0:T(8,128)(2,1)} %get-tuple-element.48) | copy-start | bytes 2359300
  39.1 2.8 %copy-start.17 = (f32[4,4]{1,0:T(4,128)S(1)}, f32[4,4]{1,0:T(4,128)}, u32[]{:S(2)}) copy-start(f32[4,4]{1,0:T(4,128)} %get-tuple-element.19) | copy-start | bytes 196
  41.9 1.4 %copy-start.5 = (bf16[4,8,2,4,1536]{4,3,2,1,0:T(4,128)(2,1)S(1)}, bf16[4,8,2,4,1536]{4,3,2,1,0:T(4,128)(2,1)}, u32[]{:S(2)}) copy-start(bf16[4,8,2,4,1536]{4,3,2,1,0:T(4,128)(2,1)} %reshape.594) | copy-start | bytes 2359300
  41.9 1.4 %copy-start.16 = (f32[4,4]{1,0:T(4,128)S(1)}, f32[4,4]{1,0:T(4,128)}, u32[]{:S(2)}) copy-start(f32[4,4]{1,0:T(4,128)} %get-tuple-element.20) | copy-start | bytes 196
  53.4 1.7 %copy-start.15 = (f32[4,4]{1,0:T(4,128)S(1)}, f32[4,4]{1,0:T(4,128)}, u32[]{:S(2)}) copy-start(f32[4,4]{1,0:T(4,128)} %get-tuple-element.17) | copy-start | bytes 196
  55.1 1.4 %copy-start.1 = (f32[4,8,2,4,1,1536]{5,3,2,1,0,4:T(4,128)S(1)}, f32[4,8,2,4,1,1536]{5,3,2,1,0,4:T(4,128)}, u32[]{:S(2)}) copy-start(f32[4,8,2,4,1,1536]{5,3,2,1,0,4:T(4,128)} %convolution_bitcast_fusion.3) | copy-start | bytes 4718596
  60.4 2.1 %copy-start.14 = (f32[4,4]{1,0:T(4,128)S(1)}, f32[4,4]{1,0:T(4,128)}, u32[]{:S(2)}) copy-start(f32[4,4]{1,0:T(4,128)} %get-tuple-element.21) | copy-start | bytes 196
  62.5 1.4 %copy-start.13 = (f32[4,4]{1,0:T(4,128)S(1)}, f32[4,4]{1,0:T(4,128)}, u32[]{:S(2)}) copy-start(f32[4,4]{1,0:T(4,128)} %get-tuple-element.22) | copy-start | bytes 196
  70.4 1.7 %copy-start.4 = (f32[4,8,1,4,1,1536]{5,3,2,1,0,4:T(4,128)S(1)}, f32[4,8,1,4,1,1536]{5,3,2,1,0,4:T(4,128)}, u32[]{:S(2)}) copy-start(f32[4,8,1,4,1,1536]{5,3,2,1,0,4:T(4,128)} %get-tuple-element.78) | copy-start | bytes 2359300
  75.4 3.4 %copy-start.2 = (f32[4,8,8,1,1536]{4,2,1,0,3:T(8,128)S(1)}, f32[4,8,8,1,1536]{4,2,1,0,3:T(8,128)}, u32[]{:S(2)}) copy-start(f32[4,8,8,1,1536]{4,2,1,0,3:T(8,128)} %stack.50) | copy-start | bytes 4718596
  75.4 3.4 %copy-start.6 = (f32[4,8,8,1,47]{4,2,3,1,0:T(8,128)S(1)}, f32[4,8,8,1,47]{4,2,3,1,0:T(8,128)}, u32[]{:S(2)}) copy-start(f32[4,8,8,1,47]{4,2,3,1,0:T(8,128)} %get-tuple-element.65) | copy-start | bytes 144388
  75.4 3.4 %copy-start.7 = (f32[4,8,8,1,47]{4,2,3,1,0:T(8,128)S(1)}, f32[4,8,8,1,47]{4,2,3,1,0:T(8,128)}, u32[]{:S(2)}) copy-start(f32[4,8,8,1,47]{4,2,3,1,0:T(8,128)} %get-tuple-element.66) | copy-start | bytes 144388
  75.4 3.4 %copy-start.8 = (f32[4,8,8,1,1]{4,2,3,1,0:T(8,128)S(1)}, f32[4,8,8,1,1]{4,2,3,1,0:T(8,128)}, u32[]{:S(2)}) copy-start(f32[4,8,8,1,1]{4,2,3,1,0:T(8,128)} %get-tuple-element.59) | copy-start | bytes 3076
  75.4 3.4 %copy-start.12 = (f32[1536]{0:T(1024)S(1)}, f32[1536]{0:T(1024)}, u32[]{:S(2)}) copy-start(f32[1536]{0:T(1024)} %get-tuple-element.71) | copy-start | bytes 18436
  75.4 3.4 %copy-start.18 = (pred[1536]{0:T(1024)(128)(4,1)S(1)}, pred[1536]{0:T(1024)(128)(4,1)}, u32[]{:S(2)}) copy-start(pred[1536]{0:T(1024)(128)(4,1)} %get-tuple-element.84) | copy-start | bytes 4612
  75.4 3.4 %copy-start.19 = (pred[1536]{0:T(1024)(128)(4,1)S(1)}, pred[1536]{0:T(1024)(128)(4,1)}, u32[]{:S(2)}) copy-start(pred[1536]{0:T(1024)(128)(4,1)} %get-tuple-element.85) | copy-start | bytes 4612
  93.0 4.2 %collective-permute-start.4 = (f32[4,4]{1,0:T(4,128)S(1)}, f32[4,4]{1,0:T(4,128)S(1)}, u32[]{:S(2)}, u32[]{:S(2)}) collective-permute-start(f32[4,4]{1,0:T(4,128)S(1)} %fusion.14), channel_id=1, source_target_pairs={{0,4},{4,0},{8,12},{12,8},{16,20},{20,16},{24,28},{28,24},{1,5},{5... | collective-permute-start | bytes 200 | tf_op jit(solution)/shard_map/ppermute | solution.py:116
  97.2 3.7 %collective-permute-start.5 = (f32[4,4]{1,0:T(4,128)S(1)}, f32[4,4]{1,0:T(4,128)S(1)}, u32[]{:S(2)}, u32[]{:S(2)}) collective-permute-start(f32[4,4]{1,0:T(4,128)S(1)} %add.228), channel_id=1, source_target_pairs={{0,8},{4,12},{8,0},{12,4},{16,24},{20,28},{24,16},{28,20},{1,9},{5... | collective-permute-start | bytes 200 | tf_op jit(solution)/shard_map/ppermute | solution.py:116
  100.9 4.6 %collective-permute-start.6 = (f32[4,4]{1,0:T(4,128)S(1)}, f32[4,4]{1,0:T(4,128)S(1)}, u32[]{:S(2)}, u32[]{:S(2)}) collective-permute-start(f32[4,4]{1,0:T(4,128)S(1)} %add.229), channel_id=1, source_target_pairs={{0,16},{4,20},{8,24},{12,28},{16,0},{20,4},{24,8},{28,12},{1,17},{... | collective-permute-start | bytes 200 | tf_op jit(solution)/shard_map/ppermute | solution.py:116
